TPU v7x, 128 devices: a whole 4x4x4 slice. The times are simulated.
128 devices in a mesh: sy: 4 (over y_lo, core), sx: 4 (over x), ch: 8 (over z, y_hi).
Axes of the slice: x: 4, y: 4 (y_hi: 2, y_lo: 2; y = y_hi * 2 + y_lo), z: 4, core: 2. Of those that a mesh axis runs over, the one named last changes fastest.
Arguments:
- frames: bfloat16 [144, 144, 128], P('sy', 'sx'), may hold values from -6 to 6
- w_input: bfloat16 [9, 64, 4, 1024], P(None, None, None, 'ch'), may hold values from -0.25 to 0.25
- w_hidden: bfloat16 [9, 1024, 4, 1024], P(None, None, None, 'ch'), may hold values from -0.0625 to 0.0625
- biases: float32 [4, 1024], P(None, 'ch'), may hold values from -4 to 4
- hidden_init: bfloat16 [144, 144, 1024], P('sy', 'sx', 'ch'), may hold values from -1 to 1
- cell_init: float32 [144, 144, 1024], P('sy', 'sx', 'ch'), may hold values from -5 to 5
Outputs:
- hidden_out: bfloat16 [144, 144, 1024], P('sy', 'sx', 'ch')
- cell_out: float32 [144, 144, 1024], P('sy', 'sx', 'ch')
All inputs are finite; a program needn't handle non-finite values.
Results may differ from a plain program's by a relative error of at most 0.0021.
Values may be sent and summed in bfloat16 or wider, within the bound.
A program may use at most 192 MiB of HBM per device.

v0:
```python
import functools

import jax
import jax.numpy as jnp
from jax import lax
from jax.experimental import pallas as pl
from jax.experimental.pallas import tpu as pltpu
from jax.sharding import PartitionSpec as P

F32 = jnp.float32
BF = jnp.bfloat16
MESH = pl.DeviceIdType.MESH

ROWS = 36
PITCH = ROWS + 2
PAD_ROWS = 1456
OUT_ROWS = 1376
SENT = (800, 752)
DONE = (720, 672)
TILES = ((144, 328), (168, 176))
TAPS = [dy * PITCH + dx for dy in range(3) for dx in range(3)]
HALO = [(dy, dx) for dy in (-1, 0, 1) for dx in (-1, 0, 1) if (dy, dx) != (0, 0)]
STRIP = 48


def sigmoid(x):
    return 0.5 * jnp.tanh(0.5 * x) + 0.5


def kernel(
    frames, w_in, w_hid, bias_in, hid_in, cell_in, hid_out, cell_out,
    fr_v, hid_v, cell_v, bias_v, raw_in, raw, wts, wts_in, spread,
    hid_p, fr_p, fr_pair, gathered, window, total, cell, strip_out, strip_in,
    hid_o, cell_o,
    load_sem, halo_send, halo_recv, send_sem, recv_sem, store_sem,
):
    sy, sx, ch = lax.axis_index("sy"), lax.axis_index("sx"), lax.axis_index("ch")
    z, half = ch // 2, ch % 2
    odd = sy % 2
    turn = 1 - 2 * odd

    def y_of(r):
        return r + odd * (ROWS - 1 - 2 * r)

    def at(dy=0, dx=0, dz=0, other=0):
        return (
            lax.rem(sy + dy * turn + 4, 4),
            lax.rem(sx + dx + 4, 4),
            lax.rem(z + dz + 4, 4) * 2 + lax.rem(half + other, 2),
        )

    def load(source, target, k):
        return pltpu.make_async_copy(source, target, load_sem.at[k])

    places = [(0, 0), (0, 1), (1, 0), (3, 0), (1, 1), (3, 1), (2, 0), (2, 1)]
    loads = [
        load(hid_in, hid_v, 0), load(frames, fr_v, 1), load(w_in, raw_in, 2),
    ]
    for j, (dz, other) in enumerate(places):
        c = lax.rem(z + dz, 4) * 2 + lax.rem(half + other, 2)
        first = pl.multiple_of(c * 512, 512)
        loads.append(load(w_hid.at[:, pl.ds(first, 512)], raw.at[j], 3 + j))
    loads += [load(cell_in, cell_v, 11), load(bias_in, bias_v, 12)]
    for copy in loads:
        copy.start()

    partners = [at(dy, dx) for dy, dx in HALO] + [at(dz=1), at(dz=-1), at(other=1)]
    barrier = pltpu.get_barrier_semaphore()
    for partner in partners:
        pl.semaphore_signal(barrier, inc=1, device_id=partner, device_id_type=MESH)

    for ref in (hid_p, fr_p):
        ref[pl.ds(0, 40), :] = jnp.zeros((40, 128), F32)
        ref[pl.ds(1400, PAD_ROWS + 8 - 1400), :] = jnp.zeros((PAD_ROWS + 8 - 1400, 128), F32)
    loads[0].wait()
    for y in range(ROWS):
        hid_p[pl.ds(PITCH * (y + 1) + 1, ROWS), :] = hid_v[y_of(y)].astype(F32)
    loads[1].wait()
    for y in range(ROWS):
        fr_p[pl.ds(PITCH * (y + 1) + 1, ROWS), :] = fr_v[y_of(y)].astype(F32)

    def edge(dy, dx, lo, hi, mine):
        def pick(d):
            if mine:
                return {-1: 1, 1: ROWS}[d]
            return {-1: 0, 1: ROWS + 1}[d]

        if dy == 0:
            return (lo + 1) * PITCH + pick(dx), hi - lo, PITCH
        if dx == 0:
            return pick(dy) * PITCH + 1, ROWS, 1
        return pick(dy) * PITCH + pick(dx), 1, 1

    def rows_of(ref, first, count, stride):
        if stride == 1:
            return ref.at[pl.ds(first, count), :]
        return ref.at[pl.ds(first, count, stride=stride), :]

    def halo_copy(e, k, there):
        dy, dx = HALO[k]
        part = (pl.ds(0, 2 if e == 0 else 1), pl.ds(0, STRIP if dy == 0 or dx == 0 else 16))
        source, target = (HALO.index((dy, -dx)), k) if there else (k, HALO.index((dy, -dx)))
        return pltpu.make_async_remote_copy(
            src_ref=strip_out.at[(e, source) + part],
            dst_ref=strip_in.at[(e, target) + part],
            send_sem=halo_send.at[e, source],
            recv_sem=halo_recv.at[e, target],
            device_id=at(dy, dx),
            device_id_type=MESH,
        )

    def sides(band):
        return [
            k for k, (dy, _) in enumerate(HALO)
            if band is None or dy == 0 or (dy == -1) == (band == 0)
        ]

    def column(band):
        return {None: (0, ROWS), 0: (0, 19), 1: (18, ROWS)}[band]

    def halo_start(e, band, fields):
        lo, hi = column(band)
        for k in sides(band):
            dy, dx = HALO[k]
            first, count, stride = edge(dy, dx, lo, hi, True)
            for f, ref in enumerate(fields):
                strip_out[e, k, f, pl.ds(0, count), :] = rows_of(ref, first, count, stride)[...].astype(BF)
            halo_copy(e, k, False).start()

    def halo_finish(e, band, fields):
        lo, hi = column(band)
        for k in sides(band):
            dy, dx = HALO[k]
            halo_copy(e, k, True).wait_recv()
            inside = jnp.where(
                ((sy + dy * turn >= 0) & (sy + dy * turn < 4)) & ((sx + dx >= 0) & (sx + dx < 4)), 1.0, 0.0
            ).astype(F32)
            first, count, stride = edge(dy, dx, lo, hi, False)
            for f, ref in enumerate(fields):
                got = strip_in[e, k, f, pl.ds(0, count), :].astype(F32) * inside
                rows_of(ref, first, count, stride)[...] = got

    def bounds(s, b):
        lo, hi = ((0, SENT[s]), (SENT[s], PAD_ROWS))[b]
        middle = lo + (hi - lo) // 32 * 16
        return lo, middle, hi

    def piece(s, b, i):
        lo, middle, hi = bounds(s, b)
        whole, one, two = (lo, hi - lo), (lo, middle - lo), (middle, hi - middle)
        up, down, across = at(dz=1), at(dz=-1), at(other=1)
        return [
            (0, 1, whole, across),
            (0, 3, whole, up),
            (0, 2, whole, down),
            (3, 6, one, up),
            (2, 6, two, down),
            (1, 5, whole, up),
            (1, 4, whole, down),
            (6, 7, one, across),
            (6, 7, two, across),
        ][i]

    def gather_copy(s, b, i):
        here, there, (first, count), target = piece(s, b, i)
        return pltpu.make_async_remote_copy(
            src_ref=gathered.at[s, here, pl.ds(first, count)],
            dst_ref=gathered.at[s, there, pl.ds(first, count)],
            send_sem=send_sem.at[s, b, i],
            recv_sem=recv_sem.at[s, b, i],
            device_id=target,
            device_id_type=MESH,
        )

    def send(s, b, *pieces):
        for i in pieces:
            gather_copy(s, b, i).start()

    def arrived(s, b, *pieces):
        for i in pieces:
            gather_copy(s, b, i).wait_recv()

    def own_band(s, b):
        lo, _, hi = bounds(s, b)
        gathered[s, 0, pl.ds(lo, hi - lo), :] = hid_p[pl.ds(lo, hi - lo), :].astype(BF)
        send(s, b, 1, 2, 0)

    def event(s, b, n):
        if n == 0:
            arrived(s, b, 1, 2)
            send(s, b, 3, 4)
            arrived(s, b, 0)
            send(s, b, 5, 6)
        elif n == 1:
            arrived(s, b, 3, 4)
            send(s, b, 7, 8)
        elif n == 2:
            arrived(s, b, 5, 6)
        elif n == 3:
            arrived(s, b, 7, 8)

    def relay(q):
        def unit(u, _):
            tap = u % 9
            spread[...] = raw[2 * q + u // 9, tap + odd * (6 - 6 * (tap // 3))].astype(F32)
            for g in range(4):
                wts[q, pl.ds(pl.multiple_of(u * 128, 128), 128), pl.ds(g * 128, 128)] = spread[
                    pl.ds(g, 128, stride=4), :
                ].astype(BF)
            return 0

        lax.fori_loop(0, 18, unit, 0)

    def relay_input():
        for dy in range(3):
            for dx in range(3):
                spread[pl.ds(0, 256), :] = raw_in[3 * (dy + odd * (2 - 2 * dy)) + dx].astype(F32)
                for g in range(4):
                    wts_in[pl.ds(dy * 256 + dx * 64, 64), pl.ds(g * 128, 128)] = spread[
                        pl.ds(g, 64, stride=4), :
                    ].astype(BF)
            wts_in[pl.ds(dy * 256 + 192, 64), :] = jnp.zeros((64, 512), BF)

    def frames_part(s, b):
        lo, count = ((0, DONE[s]), (DONE[s], OUT_ROWS - DONE[s]))[b]
        lhs = jnp.concatenate(
            [
                fr_pair[s, pl.ds(lo + dy * PITCH + dx, count), :].astype(BF)
                for dy in range(3)
                for dx in (0, 2)
            ],
            axis=1,
        )
        total[pl.ds(lo, count), :] = jnp.dot(lhs, wts_in[...], preferred_element_type=F32)

    def hidden_part(s, b, q):
        lo, count = ((0, DONE[s]), (DONE[s], OUT_ROWS - DONE[s]))[b]
        reach = (SENT[s], PAD_ROWS - DONE[s])[b]
        for p in range(2):
            window[p, pl.ds(0, reach), :] = gathered[s, 2 * q + p, pl.ds(lo, reach), :].astype(F32)
        lhs = jnp.concatenate(
            [window[p, pl.ds(tap, count), :].astype(BF) for p in range(2) for tap in TAPS], axis=1
        )
        total[pl.ds(lo, count), :] += jnp.dot(lhs, wts[q], preferred_element_type=F32)

    def gates_part(s, b):
        lo, count = ((0, DONE[s]), (DONE[s], OUT_ROWS - DONE[s]))[b]
        tile = TILES[s][b]

        def one(i, _):
            first = pl.multiple_of(lo + i * tile, 8)
            gate = [
                total[pl.ds(first, tile), pl.ds(g * 128, 128)] + bias_v[pl.ds(g, 1), :]
                for g in range(4)
            ]
            new = sigmoid(gate[1]) * cell[pl.ds(first, tile), :] + sigmoid(gate[0]) * jnp.tanh(gate[3])
            cell[pl.ds(first, tile), :] = new
            hid_p[pl.ds(first + PITCH + 1, tile), :] = sigmoid(gate[2]) * jnp.tanh(new)
            return 0

        lax.fori_loop(0, count // tile, one, 0)

    both = (hid_p, fr_p)
    pl.semaphore_wait(barrier, len(partners))
    halo_start(0, None, both)
    loads[2].wait()
    relay_input()
    halo_finish(0, None, both)
    own_band(0, 0)
    own_band(0, 1)

    lane = lax.broadcasted_iota(jnp.int32, (104, 128), 1)

    def pair_up(i, _):
        first = pl.multiple_of(i * 104, 8)
        here = fr_p[pl.ds(first, 104), :]
        there = fr_p[pl.ds(first + 1, 104), :]
        fr_pair[0, pl.ds(first, 104), :] = jnp.where(lane < 64, here, pltpu.roll(there, 64, 1))
        fr_pair[1, pl.ds(first, 104), :] = jnp.where(lane < 64, pltpu.roll(here, 64, 1), there)
        return 0

    lax.fori_loop(0, PAD_ROWS // 104, pair_up, 0)

    cell[...] = jnp.zeros_like(cell)
    loads[11].wait()
    loads[12].wait()
    for y in range(ROWS):
        cell[pl.ds(PITCH * y, ROWS), :] = cell_v[y_of(y)]
    for j in range(8):
        loads[3 + j].wait()
    for q in range(4):
        relay(q)

    def band(s, b, before):
        frames_part(s, b)

        def part(q, _):
            for n in range(4):
                @pl.when(q == n)
                def _():
                    for act in before[n]:
                        act()
            hidden_part(s, b, q)
            return 0

        lax.fori_loop(0, 4, part, 0)
        gates_part(s, b)

    def ev(s, b, n):
        return functools.partial(event, s, b, n)

    def next_band(b):
        halo_start(1 + b, b, (hid_p,))

    def next_out(b):
        halo_finish(1 + b, b, (hid_p,))
        own_band(1, b)

    nothing = ()
    band(0, 0, [[ev(0, 0, 0)], [], [ev(0, 0, 1), ev(0, 1, 0), ev(0, 0, 2)], [ev(0, 0, 3)]])
    next_band(0)
    band(0, 1, [
        [ev(0, 1, 1)], [functools.partial(next_out, 0)], [ev(0, 1, 2)], [ev(0, 1, 3)],
    ])
    next_band(1)
    next_out(1)
    band(1, 0, [[ev(1, 0, 0)], [], [ev(1, 0, 1), ev(1, 1, 0), ev(1, 0, 2)], [ev(1, 0, 3)]])

    def finish(first, last):
        for r in range(first, last):
            hid_o[y_of(r)] = hid_p[pl.ds(PITCH * (r + 1) + 1, ROWS), :].astype(BF)
            cell_o[y_of(r)] = cell[pl.ds(PITCH * r, ROWS), :]
        rows = pl.ds(first + odd * (ROWS - last - first), last - first)
        k = int(first > 0)
        copies = [
            pltpu.make_async_copy(hid_o.at[rows], hid_out.at[rows], store_sem.at[0, k]),
            pltpu.make_async_copy(cell_o.at[rows], cell_out.at[rows], store_sem.at[1, k]),
        ]
        for copy in copies:
            copy.start()
        return copies

    ends = finish(0, 17)
    band(1, 1, [[ev(1, 1, 1)], [], [ev(1, 1, 2)], [ev(1, 1, 3)]])
    ends += finish(17, ROWS)

    for k in range(8):
        halo_copy(0, k, False).wait_send()
    for b in range(2):
        for k in sides(b):
            halo_copy(1 + b, k, False).wait_send()
    for s in range(2):
        for b in range(2):
            for i in range(9):
                gather_copy(s, b, i).wait_send()
    for copy in ends:
        copy.wait()


def per_device(frames, w_input, w_hidden, biases, hidden_init, cell_init):
    w_in = w_input.reshape(9, 256, 128)
    w_hid = w_hidden.reshape(9, 4096, 128)
    dma = pltpu.SemaphoreType.DMA
    return pl.pallas_call(
        kernel,
        out_shape=(
            jax.ShapeDtypeStruct((ROWS, ROWS, 128), BF),
            jax.ShapeDtypeStruct((ROWS, ROWS, 128), F32),
        ),
        in_specs=[pl.BlockSpec(memory_space=pl.ANY)] * 6,
        out_specs=(pl.BlockSpec(memory_space=pl.ANY),) * 2,
        scratch_shapes=[
            pltpu.VMEM((ROWS, ROWS, 128), BF),
            pltpu.VMEM((ROWS, ROWS, 128), BF),
            pltpu.VMEM((ROWS, ROWS, 128), F32),
            pltpu.VMEM((4, 128), F32),
            pltpu.VMEM((9, 256, 128), BF),
            pltpu.VMEM((8, 9, 512, 128), BF),
            pltpu.VMEM((4, 2304, 512), BF),
            pltpu.VMEM((768, 512), BF),
            pltpu.VMEM((512, 128), F32),
            pltpu.VMEM((PAD_ROWS + 8, 128), F32),
            pltpu.VMEM((PAD_ROWS + 8, 128), F32),
            pltpu.VMEM((2, PAD_ROWS, 128), F32),
            pltpu.VMEM((2, 8, PAD_ROWS, 128), BF),
            pltpu.VMEM((2, SENT[0], 128), F32),
            pltpu.VMEM((OUT_ROWS, 512), F32),
            pltpu.VMEM((OUT_ROWS, 128), F32),
            pltpu.VMEM((3, 8, 2, STRIP, 128), BF),
            pltpu.VMEM((3, 8, 2, STRIP, 128), BF),
            pltpu.VMEM((ROWS, ROWS, 128), BF),
            pltpu.VMEM((ROWS, ROWS, 128), F32),
            dma((13,)),
            dma((3, 8)),
            dma((3, 8)),
            dma((2, 2, 9)),
            dma((2, 2, 9)),
            dma((2, 2)),
        ],
        compiler_params=pltpu.CompilerParams(
            collective_id=0, has_side_effects=True, vmem_limit_bytes=60 * 1024 * 1024
        ),
        name="conv_lstm",
    )(frames, w_in, w_hid, biases, hidden_init, cell_init)


def solution(mesh):
    in_specs = (
        P("sy", "sx", None),
        P(None, None, None, "ch"),
        P(None, None, None, "ch"),
        P(None, "ch"),
        P("sy", "sx", "ch"),
        P("sy", "sx", "ch"),
    )
    out_specs = (P("sy", "sx", "ch"), P("sy", "sx", "ch"))
    return jax.shard_map(
        per_device, mesh=mesh, in_specs=in_specs, out_specs=out_specs, check_vma=False
    )
```

profile of v0, /device:TPU:0, one launch (start us, length us, event | category | flops | bytes accessed | tf_op | source)
XLA Modules:
  0.0 76.8 jit_solution(4057903984639974509)
XLA Ops:
  0.6 72.3 %conv_lstm.1 = (bf16[36,36,128]{2,1,0:T(8,128)(2,1)}, f32[36,36,128]{2,1,0:T(8,128)}) custom-call(bf16[36,36,128]{2,1,0:T(8,128)(2,1)} %frames.1, bf16[9,256,128]{2,1,0:T(8,128)(2,1)} %bitcast.3, bf16[9,4096,128]{2,1,0:T(8,128)(2,1)} %bitcast.2, f32[4,128]{1,0:T(4,128)} %bias_in.1, bf16[36,36,128]{2,1,0:T(8,128)(2,1)} %hid_in.1, f32[36,36,128]{2,1,0:T(8,128)} %cell_in.1), custom_call_target="tpu_custom_call" | custom-call | tf_op jit(solution)/shard_map/conv_lstm/pallas_call | solution.py:364
  73.0 1.8 %copy.10 = bf16[36,36,128]{2,1,0:T(8,128)(2,1)} copy(bf16[36,36,128]{2,1,0:T(8,128)(2,1)} %get-tuple-element.4) | data formatting | bytes 663552
  74.7 2.0 %copy.11 = f32[36,36,128]{2,1,0:T(8,128)} copy(f32[36,36,128]{2,1,0:T(8,128)} %get-tuple-element.5) | data formatting | bytes 1327104
where the time goes:
time: 76.9 us; the launch traced here: 76.8 us
  Pallas kernels  72.3 us (94%)
  local copies, waits for them, and re-layouts  3.78 us (5%)
    pallas_call x1, Pallas kernels, per_device(): pl.pallas_call(kernel, out_shape=(jax.ShapeDtypeStruct((ROWS, ROWS, 128),...  72.3 us
    unnamed x2, local copies, waits for them, and re-layouts  3.78 us

commit v1 on v0

--- a/solution.py
+++ b/solution.py
@@ -21,6 +21,8 @@
 TAPS = [dy * PITCH + dx for dy in range(3) for dx in range(3)]
 HALO = [(dy, dx) for dy in (-1, 0, 1) for dx in (-1, 0, 1) if (dy, dx) != (0, 0)]
 STRIP = 48
+CELLS = 20
+TAIL = (128, 112)
 
 
 def sigmoid(x):
@@ -31,8 +33,8 @@
     frames, w_in, w_hid, bias_in, hid_in, cell_in, hid_out, cell_out,
     fr_v, hid_v, cell_v, bias_v, raw_in, raw, wts, wts_in, spread,
     hid_p, fr_p, fr_pair, gathered, window, total, cell, strip_out, strip_in,
-    hid_o, cell_o,
-    load_sem, halo_send, halo_recv, send_sem, recv_sem, store_sem,
+    hid_f, packs, pack_f,
+    load_sem, halo_send, halo_recv, send_sem, recv_sem, pack_send, pack_recv, store_sem,
 ):
     sy, sx, ch = lax.axis_index("sy"), lax.axis_index("sx"), lax.axis_index("ch")
     z, half = ch // 2, ch % 2
@@ -70,8 +72,7 @@
         pl.semaphore_signal(barrier, inc=1, device_id=partner, device_id_type=MESH)
 
     for ref in (hid_p, fr_p):
-        ref[pl.ds(0, 40), :] = jnp.zeros((40, 128), F32)
-        ref[pl.ds(1400, PAD_ROWS + 8 - 1400), :] = jnp.zeros((PAD_ROWS + 8 - 1400, 128), F32)
+        ref[...] = jnp.zeros_like(ref)
     loads[0].wait()
     for y in range(ROWS):
         hid_p[pl.ds(PITCH * (y + 1) + 1, ROWS), :] = hid_v[y_of(y)].astype(F32)
@@ -116,50 +117,70 @@
         ]
 
     def column(band):
-        return {None: (0, ROWS), 0: (0, 19), 1: (18, ROWS)}[band]
-
-    def halo_start(e, band, fields):
+        return {None: (0, ROWS), 0: (0, CELLS), 1: (ROWS - CELLS, ROWS)}[band]
+
+    def halo_fill(e, band, fields):
         lo, hi = column(band)
         for k in sides(band):
             dy, dx = HALO[k]
             first, count, stride = edge(dy, dx, lo, hi, True)
             for f, ref in enumerate(fields):
                 strip_out[e, k, f, pl.ds(0, count), :] = rows_of(ref, first, count, stride)[...].astype(BF)
+
+    def halo_start(e, band):
+        for k in sides(band):
             halo_copy(e, k, False).start()
 
-    def halo_finish(e, band, fields):
-        lo, hi = column(band)
+    def inside(k):
+        dy, dx = HALO[k]
+        ok = ((sy + dy * turn >= 0) & (sy + dy * turn < 4)) & ((sx + dx >= 0) & (sx + dx < 4))
+        return jnp.where(ok, 1.0, 0.0).astype(F32)
+
+    def halo_finish(e, s, band):
         for k in sides(band):
-            dy, dx = HALO[k]
             halo_copy(e, k, True).wait_recv()
-            inside = jnp.where(
-                ((sy + dy * turn >= 0) & (sy + dy * turn < 4)) & ((sx + dx >= 0) & (sx + dx < 4)), 1.0, 0.0
-            ).astype(F32)
-            first, count, stride = edge(dy, dx, lo, hi, False)
-            for f, ref in enumerate(fields):
-                got = strip_in[e, k, f, pl.ds(0, count), :].astype(F32) * inside
-                rows_of(ref, first, count, stride)[...] = got
+        for b in (0, 1) if band is None else (band,):
+            skip = 0 if band is not None else column(b)[0]
+
+            def got(dy, dx, first, count):
+                k = HALO.index((dy, dx))
+                return strip_in[e, k, 0, pl.ds(first, count), :].astype(F32) * inside(k)
+
+            edge_dy = 2 * b - 1
+            pack_f[0, pl.ds(0, CELLS), :] = got(0, -1, skip, CELLS)
+            pack_f[0, pl.ds(CELLS, CELLS), :] = got(0, 1, skip, CELLS)
+            pack_f[0, pl.ds(2 * CELLS, 1), :] = got(edge_dy, -1, 0, 1)
+            pack_f[0, pl.ds(2 * CELLS + 1, ROWS), :] = got(edge_dy, 0, 0, ROWS)
+            pack_f[0, pl.ds(2 * CELLS + 1 + ROWS, 1), :] = got(edge_dy, 1, 0, 1)
+            packs[s, 0, b] = pack_f[0].astype(BF)
+
+    def frames_halo():
+        for k, (dy, dx) in enumerate(HALO):
+            first, count, stride = edge(dy, dx, 0, ROWS, False)
+            rows_of(fr_p, first, count, stride)[...] = (
+                strip_in[0, k, 1, pl.ds(0, count), :].astype(F32) * inside(k)
+            )
 
     def bounds(s, b):
-        lo, hi = ((0, SENT[s]), (SENT[s], PAD_ROWS))[b]
+        lo, hi = ((32, SENT[s]), (SENT[s], 1408))[b]
         middle = lo + (hi - lo) // 32 * 16
         return lo, middle, hi
 
     def piece(s, b, i):
         lo, middle, hi = bounds(s, b)
-        whole, one, two = (lo, hi - lo), (lo, middle - lo), (middle, hi - middle)
+        cut = hi - TAIL[b]
+        one, two = (lo, middle - lo), (middle, hi - middle)
+        most, tail = (lo, cut - lo), (cut, hi - cut)
         up, down, across = at(dz=1), at(dz=-1), at(other=1)
         return [
-            (0, 1, whole, across),
-            (0, 3, whole, up),
-            (0, 2, whole, down),
-            (3, 6, one, up),
-            (2, 6, two, down),
-            (1, 5, whole, up),
-            (1, 4, whole, down),
-            (6, 7, one, across),
-            (6, 7, two, across),
+            (0, 1, one, across), (0, 3, one, up), (0, 2, one, down),
+            (0, 1, two, across), (0, 3, two, up), (0, 2, two, down),
+            (3, 6, one, up), (2, 6, two, down),
+            (1, 5, most, up), (1, 4, most, down), (2, 4, tail, across), (3, 5, tail, across),
+            (6, 7, one, across), (6, 7, two, across),
         ][i]
+
+    FIRST, SECOND, AHEAD, ROUND, TAILS, CROSS = (1, 2, 0), (4, 5, 3), (6, 7), (8, 9), (10, 11), (12, 13)
 
     def gather_copy(s, b, i):
         here, there, (first, count), target = piece(s, b, i)
@@ -172,32 +193,48 @@
             device_id_type=MESH,
         )
 
-    def send(s, b, *pieces):
-        for i in pieces:
-            gather_copy(s, b, i).start()
-
-    def arrived(s, b, *pieces):
-        for i in pieces:
-            gather_copy(s, b, i).wait_recv()
+    def send(s, b, *groups):
+        for group in groups:
+            for i in group:
+                gather_copy(s, b, i).start()
+
+    def arrived(s, b, *groups):
+        for group in groups:
+            for i in group:
+                gather_copy(s, b, i).wait_recv()
+
+    def pack_copy(s, b, i):
+        up, down, across = at(dz=1), at(dz=-1), at(other=1)
+        here, there, target = [
+            (0, 1, across), (0, 3, up), (0, 2, down),
+            ((3, 6, up), (2, 6, down))[b],
+            (1, 5, up), (1, 4, down),
+            (6, 7, across),
+        ][i]
+        return pltpu.make_async_remote_copy(
+            src_ref=packs.at[s, here, b],
+            dst_ref=packs.at[s, there, b],
+            send_sem=pack_send.at[s, b, i],
+            recv_sem=pack_recv.at[s, b, i],
+            device_id=target,
+            device_id_type=MESH,
+        )
+
+    PACK_OWN, PACK_AHEAD, PACK_ROUND, PACK_CROSS = (1, 2, 0), (3,), (4, 5), (6,)
+
+    def pack_send_on(s, b, *groups):
+        for group in groups:
+            for i in group:
+                pack_copy(s, b, i).start()
+
+    def pack_arrived(s, b, *groups):
+        for group in groups:
+            for i in group:
+                pack_copy(s, b, i).wait_recv()
 
     def own_band(s, b):
         lo, _, hi = bounds(s, b)
         gathered[s, 0, pl.ds(lo, hi - lo), :] = hid_p[pl.ds(lo, hi - lo), :].astype(BF)
-        send(s, b, 1, 2, 0)
-
-    def event(s, b, n):
-        if n == 0:
-            arrived(s, b, 1, 2)
-            send(s, b, 3, 4)
-            arrived(s, b, 0)
-            send(s, b, 5, 6)
-        elif n == 1:
-            arrived(s, b, 3, 4)
-            send(s, b, 7, 8)
-        elif n == 2:
-            arrived(s, b, 5, 6)
-        elif n == 3:
-            arrived(s, b, 7, 8)
 
     def relay(q):
         def unit(u, _):
@@ -238,6 +275,19 @@
         reach = (SENT[s], PAD_ROWS - DONE[s])[b]
         for p in range(2):
             window[p, pl.ds(0, reach), :] = gathered[s, 2 * q + p, pl.ds(lo, reach), :].astype(F32)
+            pack_f[p] = packs[s, 2 * q + p, b].astype(F32)
+            for x, slot in ((0, 0), (PITCH - 1, CELLS)):
+                ys = [y for y in range(*column(b)) if lo <= PITCH * (y + 1) + x < min(lo + count + 78, PAD_ROWS)]
+                window[p, pl.ds(PITCH * (ys[0] + 1) + x - lo, len(ys), stride=PITCH), :] = pack_f[
+                    p, pl.ds(slot + ys[0] - column(b)[0], len(ys)), :
+                ]
+            if b == 1:
+                window[p, pl.ds(PITCH * PITCH - lo, PAD_ROWS - PITCH * PITCH), :] = jnp.zeros(
+                    (PAD_ROWS - PITCH * PITCH, 128), F32
+                )
+            window[p, pl.ds((0, PITCH * (PITCH - 1) - lo)[b], PITCH), :] = pack_f[
+                p, pl.ds(2 * CELLS, PITCH), :
+            ]
         lhs = jnp.concatenate(
             [window[p, pl.ds(tap, count), :].astype(BF) for p in range(2) for tap in TAPS], axis=1
         )
@@ -255,19 +305,23 @@
             ]
             new = sigmoid(gate[1]) * cell[pl.ds(first, tile), :] + sigmoid(gate[0]) * jnp.tanh(gate[3])
             cell[pl.ds(first, tile), :] = new
-            hid_p[pl.ds(first + PITCH + 1, tile), :] = sigmoid(gate[2]) * jnp.tanh(new)
+            if s == 0:
+                hid_p[pl.ds(first + PITCH + 1, tile), :] = sigmoid(gate[2]) * jnp.tanh(new)
+            else:
+                hid_f[pl.ds(first, tile), :] = sigmoid(gate[2]) * jnp.tanh(new)
             return 0
 
         lax.fori_loop(0, count // tile, one, 0)
 
     both = (hid_p, fr_p)
+    own_band(0, 0)
+    halo_fill(0, None, both)
+    own_band(0, 1)
     pl.semaphore_wait(barrier, len(partners))
-    halo_start(0, None, both)
+    halo_start(0, None)
+    send(0, 0, FIRST, SECOND)
     loads[2].wait()
     relay_input()
-    halo_finish(0, None, both)
-    own_band(0, 0)
-    own_band(0, 1)
 
     lane = lax.broadcasted_iota(jnp.int32, (104, 128), 1)
 
@@ -279,8 +333,6 @@
         fr_pair[1, pl.ds(first, 104), :] = jnp.where(lane < 64, pltpu.roll(here, 64, 1), there)
         return 0
 
-    lax.fori_loop(0, PAD_ROWS // 104, pair_up, 0)
-
     cell[...] = jnp.zeros_like(cell)
     loads[11].wait()
     loads[12].wait()
@@ -288,61 +340,118 @@
         cell[pl.ds(PITCH * y, ROWS), :] = cell_v[y_of(y)]
     for j in range(8):
         loads[3 + j].wait()
-    for q in range(4):
-        relay(q)
-
-    def band(s, b, before):
-        frames_part(s, b)
-
-        def part(q, _):
-            for n in range(4):
-                @pl.when(q == n)
-                def _():
-                    for act in before[n]:
-                        act()
-            hidden_part(s, b, q)
-            return 0
-
-        lax.fori_loop(0, 4, part, 0)
-        gates_part(s, b)
-
-    def ev(s, b, n):
-        return functools.partial(event, s, b, n)
-
-    def next_band(b):
-        halo_start(1 + b, b, (hid_p,))
-
-    def next_out(b):
-        halo_finish(1 + b, b, (hid_p,))
-        own_band(1, b)
-
-    nothing = ()
-    band(0, 0, [[ev(0, 0, 0)], [], [ev(0, 0, 1), ev(0, 1, 0), ev(0, 0, 2)], [ev(0, 0, 3)]])
-    next_band(0)
-    band(0, 1, [
-        [ev(0, 1, 1)], [functools.partial(next_out, 0)], [ev(0, 1, 2)], [ev(0, 1, 3)],
-    ])
-    next_band(1)
-    next_out(1)
-    band(1, 0, [[ev(1, 0, 0)], [], [ev(1, 0, 1), ev(1, 1, 0), ev(1, 0, 2)], [ev(1, 0, 3)]])
-
-    def finish(first, last):
-        for r in range(first, last):
-            hid_o[y_of(r)] = hid_p[pl.ds(PITCH * (r + 1) + 1, ROWS), :].astype(BF)
-            cell_o[y_of(r)] = cell[pl.ds(PITCH * r, ROWS), :]
-        rows = pl.ds(first + odd * (ROWS - last - first), last - first)
-        k = int(first > 0)
+    def finish(b):
+        lo, count = ((0, DONE[1]), (DONE[1], OUT_ROWS - DONE[1]))[b]
+        rows = pl.ds(lo, count)
         copies = [
-            pltpu.make_async_copy(hid_o.at[rows], hid_out.at[rows], store_sem.at[0, k]),
-            pltpu.make_async_copy(cell_o.at[rows], cell_out.at[rows], store_sem.at[1, k]),
+            pltpu.make_async_copy(hid_f.at[rows], hid_out.at[rows], store_sem.at[0, b]),
+            pltpu.make_async_copy(cell.at[rows], cell_out.at[rows], store_sem.at[1, b]),
         ]
         for copy in copies:
             copy.start()
         return copies
 
-    ends = finish(0, 17)
-    band(1, 1, [[ev(1, 1, 1)], [], [ev(1, 1, 2)], [ev(1, 1, 3)]])
-    ends += finish(17, ROWS)
+    relay(0)
+    halo_finish(0, 0, None)
+    pack_send_on(0, 0, PACK_OWN)
+    pack_send_on(0, 1, PACK_OWN)
+    send(0, 1, FIRST, SECOND)
+    frames_halo()
+    lax.fori_loop(0, PAD_ROWS // 104, pair_up, 0)
+    relay(1)
+    relay(2)
+    relay(3)
+
+    arrived(0, 0, FIRST, SECOND)
+    send(0, 0, AHEAD, TAILS)
+    pack_arrived(0, 0, PACK_OWN)
+    pack_send_on(0, 0, PACK_AHEAD, PACK_ROUND)
+    send(0, 0, ROUND)
+    frames_part(0, 0)
+    hidden_part(0, 0, 0)
+    pack_arrived(0, 1, PACK_OWN)
+    pack_send_on(0, 1, PACK_AHEAD, PACK_ROUND)
+    arrived(0, 0, AHEAD)
+    send(0, 0, CROSS)
+    pack_arrived(0, 0, PACK_AHEAD)
+    pack_send_on(0, 0, PACK_CROSS)
+    hidden_part(0, 0, 1)
+    arrived(0, 1, FIRST, SECOND)
+    send(0, 1, AHEAD, TAILS, ROUND)
+    frames_part(0, 1)
+    hidden_part(0, 1, 0)
+    arrived(0, 0, ROUND, TAILS)
+    pack_arrived(0, 0, PACK_ROUND)
+    hidden_part(0, 0, 2)
+    arrived(0, 1, AHEAD)
+    send(0, 1, CROSS)
+    pack_arrived(0, 1, PACK_AHEAD)
+    pack_send_on(0, 1, PACK_CROSS)
+    arrived(0, 0, CROSS)
+    pack_arrived(0, 0, PACK_CROSS)
+    hidden_part(0, 0, 3)
+    gates_part(0, 0)
+    halo_fill(1, 0, (hid_p,))
+    halo_start(1, 0)
+    own_band(1, 0)
+    send(1, 0, FIRST, SECOND)
+    hidden_part(0, 1, 1)
+    arrived(0, 1, ROUND, TAILS)
+    pack_arrived(0, 1, PACK_ROUND)
+    hidden_part(0, 1, 2)
+    halo_finish(1, 1, 0)
+    pack_send_on(1, 0, PACK_OWN)
+    arrived(0, 1, CROSS)
+    pack_arrived(0, 1, PACK_CROSS)
+    hidden_part(0, 1, 3)
+    arrived(1, 0, FIRST, SECOND)
+    send(1, 0, AHEAD, TAILS)
+    gates_part(0, 1)
+    halo_fill(2, 1, (hid_p,))
+    halo_start(2, 1)
+    own_band(1, 1)
+    send(1, 1, FIRST, SECOND)
+
+    pack_arrived(1, 0, PACK_OWN)
+    pack_send_on(1, 0, PACK_AHEAD, PACK_ROUND)
+    frames_part(1, 0)
+    hidden_part(1, 0, 0)
+    halo_finish(2, 1, 1)
+    pack_send_on(1, 1, PACK_OWN)
+    send(1, 0, ROUND)
+    arrived(1, 0, AHEAD)
+    send(1, 0, CROSS)
+    hidden_part(1, 0, 1)
+    pack_arrived(1, 0, PACK_AHEAD)
+    pack_send_on(1, 0, PACK_CROSS)
+    arrived(1, 1, FIRST, SECOND)
+    send(1, 1, AHEAD, TAILS)
+    pack_arrived(1, 1, PACK_OWN)
+    pack_send_on(1, 1, PACK_AHEAD, PACK_ROUND)
+    send(1, 1, ROUND)
+    frames_part(1, 1)
+    hidden_part(1, 1, 0)
+    arrived(1, 0, ROUND, TAILS)
+    pack_arrived(1, 0, PACK_ROUND)
+    hidden_part(1, 0, 2)
+    arrived(1, 1, AHEAD)
+    send(1, 1, CROSS)
+    pack_arrived(1, 1, PACK_AHEAD)
+    pack_send_on(1, 1, PACK_CROSS)
+    arrived(1, 0, CROSS)
+    pack_arrived(1, 0, PACK_CROSS)
+    hidden_part(1, 0, 3)
+    gates_part(1, 0)
+    ends = finish(0)
+    hidden_part(1, 1, 1)
+    arrived(1, 1, ROUND, TAILS)
+    pack_arrived(1, 1, PACK_ROUND)
+    hidden_part(1, 1, 2)
+    arrived(1, 1, CROSS)
+    pack_arrived(1, 1, PACK_CROSS)
+    hidden_part(1, 1, 3)
+    gates_part(1, 1)
+    ends += finish(1)
 
     for k in range(8):
         halo_copy(0, k, False).wait_send()
@@ -351,22 +460,29 @@
             halo_copy(1 + b, k, False).wait_send()
     for s in range(2):
         for b in range(2):
-            for i in range(9):
+            for i in range(14):
                 gather_copy(s, b, i).wait_send()
+            for i in range(7):
+                pack_copy(s, b, i).wait_send()
     for copy in ends:
         copy.wait()
+
+
+def lay_out(hid_in, cell_in, hid_out, cell_out):
+    odd = lax.axis_index("sy") % 2
+    for r in range(ROWS):
+        y = r + odd * (ROWS - 1 - 2 * r)
+        hid_out[y] = hid_in[pl.ds(PITCH * r, ROWS), :].astype(BF)
+        cell_out[y] = cell_in[pl.ds(PITCH * r, ROWS), :]
 
 
 def per_device(frames, w_input, w_hidden, biases, hidden_init, cell_init):
     w_in = w_input.reshape(9, 256, 128)
     w_hid = w_hidden.reshape(9, 4096, 128)
     dma = pltpu.SemaphoreType.DMA
-    return pl.pallas_call(
+    flat = pl.pallas_call(
         kernel,
-        out_shape=(
-            jax.ShapeDtypeStruct((ROWS, ROWS, 128), BF),
-            jax.ShapeDtypeStruct((ROWS, ROWS, 128), F32),
-        ),
+        out_shape=(jax.ShapeDtypeStruct((OUT_ROWS, 128), F32),) * 2,
         in_specs=[pl.BlockSpec(memory_space=pl.ANY)] * 6,
         out_specs=(pl.BlockSpec(memory_space=pl.ANY),) * 2,
         scratch_shapes=[
@@ -388,13 +504,16 @@
             pltpu.VMEM((OUT_ROWS, 128), F32),
             pltpu.VMEM((3, 8, 2, STRIP, 128), BF),
             pltpu.VMEM((3, 8, 2, STRIP, 128), BF),
-            pltpu.VMEM((ROWS, ROWS, 128), BF),
-            pltpu.VMEM((ROWS, ROWS, 128), F32),
+            pltpu.VMEM((OUT_ROWS, 128), F32),
+            pltpu.VMEM((2, 8, 2, 80, 128), BF),
+            pltpu.VMEM((2, 80, 128), F32),
             dma((13,)),
             dma((3, 8)),
             dma((3, 8)),
-            dma((2, 2, 9)),
-            dma((2, 2, 9)),
+            dma((2, 2, 14)),
+            dma((2, 2, 14)),
+            dma((2, 2, 7)),
+            dma((2, 2, 7)),
             dma((2, 2)),
         ],
         compiler_params=pltpu.CompilerParams(
@@ -402,6 +521,16 @@
         ),
         name="conv_lstm",
     )(frames, w_in, w_hid, biases, hidden_init, cell_init)
+    return pl.pallas_call(
+        lay_out,
+        out_shape=(
+            jax.ShapeDtypeStruct((ROWS, ROWS, 128), BF),
+            jax.ShapeDtypeStruct((ROWS, ROWS, 128), F32),
+        ),
+        in_specs=[pl.BlockSpec(memory_space=pltpu.VMEM)] * 2,
+        out_specs=(pl.BlockSpec(memory_space=pltpu.VMEM),) * 2,
+        name="lay_out",
+    )(*flat)
 
 
 def solution(mesh):

time: 76.9 us -> 65.9 us (0.86)
  Pallas kernels: 72.3 us -> 65.2 us
  local copies, waits for them, and re-layouts: 3.78 us -> 0 us
    pallas_call x1 -> x2, Pallas kernels: 72.3 us -> 65.2 us  [the longest x1 62.8 us: per_device(): pl.pallas_call(kernel, out_shape=(jax.ShapeDtypeStruct((OUT_ROWS, 128), F...]
    unnamed x2 -> x0, local copies, waits for them, and re-layouts: 3.78 us -> none
where the time goes in v1:
time: 65.9 us; the launch traced here: 65.8 us
  Pallas kernels  65.2 us (99%)
    pallas_call x1, Pallas kernels, per_device(): pl.pallas_call(kernel, out_shape=(jax.ShapeDtypeStruct((OUT_ROWS, 128), F...  62.8 us
    pallas_call x1, Pallas kernels, per_device(): pl.pallas_call(lay_out, out_shape=(jax.ShapeDtypeStruct((ROWS, ROWS, 128)...  2.39 us

profile of v1, /device:TPU:0, one launch (start us, length us, event | category | flops | bytes accessed | tf_op | source)
XLA Modules:
  0.0 65.8 jit_solution(13538766657052355441)
XLA Ops:
  0.6 62.8 %conv_lstm.1 = (f32[1376,128]{1,0:T(8,128)}, f32[1376,128]{1,0:T(8,128)}) custom-call(bf16[36,36,128]{2,1,0:T(8,128)(2,1)} %frames.1, bf16[9,256,128]{2,1,0:T(8,128)(2,1)} %bitcast.3, bf16[9,4096,128]{2,1,0:T(8,128)(2,1)} %bitcast.2, f32[4,128]{1,0:T(4,128)} %bias_in.1, bf16[36,36,128]{2,1,0:T(8,128)(2,1)} %hid_in.1, f32[36,36,128]{2,1,0:T(8,128)} %cell_in.1), custom_call_target="tpu_custom_call" | custom-call | tf_op jit(solution)/shard_map/conv_lstm/pallas_call | solution.py:483
  63.4 2.4 %lay_out.1 = (bf16[36,36,128]{2,1,0:T(8,128)(2,1)}, f32[36,36,128]{2,1,0:T(8,128)}) custom-call(f32[1376,128]{1,0:T(8,128)} %get-tuple-element.4.hid_in, f32[1376,128]{1,0:T(8,128)} %get-tuple-element.5.cell_in), custom_call_target="tpu_custom_call" | custom-call | tf_op jit(solution)/shard_map/lay_out/pallas_call | solution.py:524
